TPU v7x, 256 devices: a whole 4x4x8 slice. The times are simulated.
256 devices in a mesh: dp: 2 (over x_lo), context: 8 (over z), tensor: 16 (over y, x_hi, core).
Axes of the slice: x: 4 (x_hi: 2, x_lo: 2; x = x_hi * 2 + x_lo), y: 4, z: 8, core: 2. Of those that a mesh axis runs over, the one named last changes fastest.
Arguments:
- activations: bfloat16 [2, 4096, 4096], P('dp', ('context', 'tensor')), may hold values from -60 to 60
- in_weight: bfloat16 [4096, 3, 4096], P('dp', None, 'tensor'), may hold values from -0.09375 to 0.09375
- out_weight: bfloat16 [4096, 4096], P('tensor', 'dp'), may hold values from -0.09375 to 0.09375
- short_filter: float32 [3, 3, 4096], P(None, None, 'tensor'), may hold values from -2 to 2
- mixer_filter: float32 [128, 256], P(None, 'tensor'), may hold values from -0.5 to 0.5
- cotangent: bfloat16 [2, 4096, 4096], P('dp', ('context', 'tensor')), may hold values from -6 to 6
Outputs:
- block_out: bfloat16 [2, 4096, 4096], P('dp', ('context', 'tensor'))
- grad_input: bfloat16 [2, 4096, 4096], P('dp', ('context', 'tensor'))
- grad_in_weight: bfloat16 [4096, 3, 4096], P(('dp', 'context'), None, 'tensor')
- grad_out_weight: bfloat16 [4096, 4096], P('tensor', ('dp', 'context'))
- grad_short: float32 [3, 3, 4096], P(None, None, 'tensor')
- grad_mixer: float32 [128, 256], P(None, 'tensor')
All inputs are finite; a program needn't handle non-finite values.
Results may differ from a plain program's by a relative error of at most 0.019.
Values may be sent and summed in bfloat16 or wider, within the bound.
A program may use at most 128 MiB of HBM per device.

v0:
```python
import jax
import jax.numpy as jnp
from jax import lax
from jax.sharding import PartitionSpec as P

EPS = 1e-05


def from_behind(value, axis, steps):
    count = lax.axis_size(axis)
    initial, last = (max(0, -steps), min(count, count - steps))
    return lax.ppermute(value, axis, [(source, source + steps) for source in range(initial, last)])


def pair_gather(value, axis, dim):
    count = lax.axis_size(axis)
    index = lax.axis_index(axis)
    parts = [value]
    for step in range(1, count):
        parts.append(lax.ppermute(value, axis, [(i, (i + step) % count) for i in range(count)]))
    shape = list(value.shape)
    size = shape[dim]
    shape[dim] = size * count
    full = jnp.zeros(shape, value.dtype)
    for step, part in enumerate(parts):
        start = [0] * len(shape)
        start[dim] = (index - step) % count * size
        full = lax.dynamic_update_slice(full, part, start)
    return full


def scatter_sum(value, axis, dim):
    count = lax.axis_size(axis)
    shape = value.shape
    split = shape[:dim] + (count, shape[dim] // count) + shape[dim + 1 :]
    pieces = lax.all_to_all(value.reshape(split), axis, dim, 0)
    return jnp.sum(pieces.astype(jnp.float32), axis=0)


def skew_table(base, span):
    groups = base.shape[0]
    padded = jnp.concatenate([base, jnp.zeros((groups, span + 1), jnp.float32)], axis=1)
    tiled = jnp.tile(padded[:, None, :], (1, span, 1)).reshape(groups, span * (2 * span + 1))
    return tiled[:, : span * 2 * span].reshape(groups, span, 2 * span)


def band_windows(extended, span, groups):
    chans = extended.shape[1]
    padded = jnp.concatenate([extended, jnp.zeros((1, chans), jnp.float32)], 0)
    blocks = padded.shape[0] // span
    padded = padded.reshape(blocks, span, groups, chans // groups)
    return jnp.concatenate([padded[:-1], padded[1:]], axis=1)


def band_apply(table, extended, span):
    groups = table.shape[0]
    chans = extended.shape[1]
    windows = band_windows(extended, span, groups)
    result = jnp.einsum("gtu,bugc->btgc", table, windows, precision=lax.Precision.HIGHEST)
    return result.reshape(windows.shape[0] * span, chans)


def band_grad(left, extended, span, groups):
    rows, chans = left.shape
    lhs = left.reshape(rows // span, span, groups, chans // groups)
    windows = band_windows(extended, span, groups)
    prods = jnp.einsum("btgc,bugc->gtu", lhs, windows, precision=lax.Precision.HIGHEST)
    flat = jnp.concatenate(
        [prods.reshape(groups, span * 2 * span), jnp.zeros((groups, span), jnp.float32)], axis=1
    )
    skewed = flat.reshape(groups, span, 2 * span + 1).sum(axis=1)
    return jnp.flip(skewed[:, :span], axis=1).T


def short_apply(filters, extended, rows):
    taps = filters.shape[1]
    total = jnp.zeros((rows,) + extended.shape[1:], jnp.float32)
    for tap in range(taps):
        total = total + filters[:, tap][None] * extended[taps - 1 - tap : taps - 1 - tap + rows]
    return total


def per_device(activations, in_weight, out_weight, short_filter, mixer_filter, cotangent):
    rows_own = activations.shape[1]
    width = activations.shape[2]
    rows = rows_own * lax.axis_size("tensor")
    span = mixer_filter.shape[0]
    groups = mixer_filter.shape[1]
    taps = short_filter.shape[1]
    chans = short_filter.shape[2]
    own = activations[0].astype(jnp.float32)
    inverse = lax.rsqrt(jnp.mean(own * own, axis=-1, keepdims=True) + EPS)
    normed = (own * inverse).astype(jnp.bfloat16)
    slab = lax.all_gather(normed, "tensor", axis=0, tiled=True)
    full_in = pair_gather(in_weight, "dp", 0)
    full_out = pair_gather(out_weight, "dp", 1)
    in_flat = full_in.reshape(width, 3 * chans)
    projected = (
        jnp.dot(slab, in_flat, preferred_element_type=jnp.float32)
        .astype(jnp.bfloat16)
        .reshape(rows, 3, chans)
    )
    proj_wide = projected.astype(jnp.float32)
    table_fwd = skew_table(jnp.flip(mixer_filter, axis=0).T, span)
    table_back = skew_table(mixer_filter.T, span)
    short_rim = from_behind(projected[rows - taps + 1 :], "context", 1)
    proj_ext = jnp.concatenate([short_rim.astype(jnp.float32), proj_wide], 0)
    streams = short_apply(short_filter, proj_ext, rows)
    gated = (streams[:, 1] * streams[:, 2]).astype(jnp.bfloat16)
    gate_rim = from_behind(gated[rows - span + 1 :], "context", 1)
    gate_ext = jnp.concatenate([gate_rim, gated], 0).astype(jnp.float32)
    mixed = band_apply(table_fwd, gate_ext, span)
    output_rows = (streams[:, 0] * mixed).astype(jnp.bfloat16)
    piece = output_rows
    branch = scatter_sum(
        jnp.dot(piece, full_out, preferred_element_type=jnp.float32).astype(jnp.bfloat16),
        "tensor",
        0,
    )
    block_out = (own + branch).astype(jnp.bfloat16)[None]
    cot_slab = lax.all_gather(cotangent[0], "tensor", axis=0, tiled=True)
    grad_rows = lax.dot_general(
        cot_slab, full_out, (((1,), (1,)), ((), ())), preferred_element_type=jnp.float32
    )
    out_term = lax.dot_general(
        output_rows, cot_slab, (((0,), (0,)), ((), ())), preferred_element_type=jnp.float32
    )
    grad_mix = (grad_rows * streams[:, 0]).astype(jnp.bfloat16)
    grad_mix_wide = grad_mix.astype(jnp.float32)
    mix_rim = from_behind(grad_mix[: span - 1], "context", -1)
    grad_gate = band_apply(
        table_back, jnp.concatenate([grad_mix_wide, mix_rim.astype(jnp.float32)], 0), span
    )
    mixer_term = band_grad(grad_mix_wide, gate_ext, span, groups)
    grad_streams = jnp.stack(
        [grad_rows * mixed, grad_gate * streams[:, 2], grad_gate * streams[:, 1]], axis=1
    )
    stream_rim = from_behind(grad_streams[: taps - 1], "context", -1)
    stream_ext = jnp.concatenate([grad_streams, stream_rim], 0)
    grad_proj = jnp.zeros((rows, 3, chans), jnp.float32)
    for tap in range(taps):
        grad_proj = grad_proj + short_filter[:, tap][None] * stream_ext[tap : tap + rows]
    grad_proj = grad_proj.astype(jnp.bfloat16)
    short_terms = [
        jnp.sum(grad_streams * proj_ext[taps - 1 - tap : taps - 1 - tap + rows], axis=0)
        for tap in range(taps)
    ]
    short_term = jnp.stack(short_terms, axis=1)
    grad_short, grad_mixer = lax.psum((short_term, mixer_term), ("dp", "context"))
    proj_flat = grad_proj.reshape(rows, 3 * chans)
    in_term = lax.dot_general(
        slab, proj_flat, (((0,), (0,)), ((), ())), preferred_element_type=jnp.float32
    ).reshape(width, 3, chans)
    grad_in, grad_out = (
        lax.psum_scatter(
            in_term.astype(jnp.bfloat16), ("dp", "context"), scatter_dimension=0, tiled=True
        ).astype(jnp.float32),
        lax.psum_scatter(
            out_term.astype(jnp.bfloat16), ("dp", "context"), scatter_dimension=1, tiled=True
        ).astype(jnp.float32),
    )
    piece = proj_flat
    grad_norm = scatter_sum(
        lax.dot_general(
            piece, in_flat, (((1,), (1,)), ((), ())), preferred_element_type=jnp.float32
        ).astype(jnp.bfloat16),
        "tensor",
        0,
    )
    grad_x = (
        cotangent[0].astype(jnp.float32)
        + inverse * grad_norm
        - own * inverse**3 * jnp.mean(grad_norm * own, axis=-1, keepdims=True)
    )
    grad_input = grad_x.astype(jnp.bfloat16)[None]
    return (
        block_out,
        grad_input,
        grad_in.astype(jnp.bfloat16),
        grad_out.astype(jnp.bfloat16),
        grad_short,
        grad_mixer,
    )


def solution(mesh):
    placed = (
        P("dp", ("context", "tensor"), None),
        P("dp", None, "tensor"),
        P("tensor", "dp"),
        P(None, None, "tensor"),
        P(None, "tensor"),
        P("dp", ("context", "tensor"), None),
    )
    return jax.shard_map(
        per_device,
        mesh=mesh,
        in_specs=placed,
        out_specs=(
            P("dp", ("context", "tensor"), None),
            P("dp", ("context", "tensor"), None),
            P(("dp", "context"), None, "tensor"),
            P("tensor", ("dp", "context")),
            P(None, None, "tensor"),
            P(None, "tensor"),
        ),
        check_vma=False,
    )
```

profile of v0, /device:TPU:6, one launch (start us, length us, event | category | flops | bytes accessed | tf_op | source)
XLA Modules:
  0.0 470.9 jit_solution(5357234230657179776)
XLA Ops:
  11.9 4.7 %copy.21 = bf16[2048,3,256]{0,2,1:T(8,128)(2,1)} copy(bf16[2048,3,256]{2,0,1:T(8,128)(2,1)} %param.7) | data formatting | bytes 6291456 | tf_op args[1]
  23.7 3.9 constant_dynamic-update-slice_fusion.3
  27.7 74.4 %collective-permute-done = bf16[2048,3,256]{0,2,1:T(8,128)(2,1)} collective-permute-done((bf16[2048,3,256]{0,2,1:T(8,128)(2,1)}, bf16[2048,3,256]{0,2,1:T(8,128)(2,1)}, u32[]{:S(2)}, u32[]{:S(2)}) %collective-permute-start) | collective-permute-done | bytes 3145760 | tf_op jit(solution)/shard_map/ppermute | solution.py:20
  102.0 4.1 constant_dynamic-update-slice_fusion.2
  106.1 7.5 %convolution_convert_fusion.3 = bf16[512,768]{1,0:T(8,128)(2,1)S(1)} fusion(bf16[512,4096]{1,0:T(8,128)(2,1)} %all-gather.4.cloned.1.call-done, bf16[4096,768]{0,1:T(8,128)(2,1)} %bitcast.1), kind=kOutput, calls=%fused_computation.29 | convolution fusion | flops 3221618688 | bytes 11272192 | tf_op jit(solution)/shard_map/dot_general | solution.py:99
  113.9 4.5 collective-permute-start.1
  118.4 7.8 %collective-permute-done.3 = bf16[256,2048]{1,0:T(8,128)(2,1)} collective-permute-done((bf16[256,2048]{1,0:T(8,128)(2,1)}, bf16[256,2048]{1,0:T(8,128)(2,1)}, u32[]{:S(2)}, u32[]{:S(2)}) %collective-permute-start.3) | collective-permute-done | bytes 1048608 | tf_op jit(solution)/shard_map/ppermute | solution.py:20
  130.0 4.2 multiply_add_fusion
  134.3 16.4 %all-gather.6.cloned.1.call-done = bf16[1,512,4096]{2,1,0:T(8,128)(2,1)} async-done(((bf16[1,32,4096]{2,1,0:T(8,128)(2,1)}), bf16[1,512,4096]{2,1,0:T(8,128)(2,1)}) %all-gather.6.cloned.1.call-update) | async-done | bytes 4194320 | tf_op jit(solution)/shard_map/all_gather | solution.py:121
  150.6 4.5 fusion.42
  158.5 3.9 tile.17
  172.9 3.9 fusion.15
  181.0 5.2 %collective-permute-start.2 = (bf16[127,256]{0,1:T(8,128)(2,1)}, bf16[127,256]{0,1:T(8,128)(2,1)}, u32[]{:S(2)}, u32[]{:S(2)}) collective-permute-start(bf16[127,256]{0,1:T(8,128)(2,1)} %slice_bitcast_fusion.1), channel_id=1, source_target_pairs={{0,16},{16,32},{32,48},{48,64},{64,80},{80,96},{96,112},{1,17},{17... | collective-permute-start | bytes 195080 | tf_op jit(solution)/shard_map/ppermute | solution.py:12
  190.1 3.9 tile.15
  207.6 4.3 fusion.12
  220.7 12.7 %collective-permute-done.5 = f32[2,3,256]{0,2,1:T(8,128)S(1)} collective-permute-done((f32[2,3,256]{0,2,1:T(8,128)S(1)}, f32[2,3,256]{0,2,1:T(8,128)S(1)}, u32[]{:S(2)}, u32[]{:S(2)}) %collective-permute-start.5) | collective-permute-done | bytes 6176 | tf_op jit(solution)/shard_map/ppermute | solution.py:12
  233.5 3.4 multiply_reduce_fusion.1
  237.8 5.4 %convolution_convert_fusion = bf16[4096,3,256]{2,0,1:T(8,128)(2,1)} fusion(bf16[512,4096]{1,0:T(8,128)(2,1)S(1)} %copy-done.25, bf16[512,3,256]{0,2,1:T(8,128)(2,1)S(1)} %get-tuple-element.20), kind=kOutput, calls=%fused_computation.3 | convolution fusion | flops 3224371200 | bytes 11272192 | tf_op jit(solution)/shard_map/dot_general | solution.py:151
  247.5 6.9 %all-to-all-start = ((bf16[16,32,4096]{2,1,0:T(8,128)(2,1)}), bf16[16,32,4096]{2,1,0:T(8,128)(2,1)}, u32[]{:S(2)}, u32[]{:S(2)}) async-start(bf16[16,32,4096]{2,1,0:T(8,128)(2,1)} %bitcast.143), calls=%async_computation | async-start | bytes 8388608 | tf_op jit(solution)/shard_map/all_to_all | solution.py:36
  254.4 7.8 %bitcast_convert_fusion = bf16[512,4096]{1,0:T(8,128)(2,1)} fusion(bf16[512,3,256]{0,2,1:T(8,128)(2,1)S(1)} %copy-done.18, bf16[4096,3,256]{0,2,1:T(8,128)(2,1)} %constant_dynamic-update-slice_fusion.2), kind=kOutput, calls=%fused_computation | convolution fusion | flops 3223322624 | bytes 11272192 | tf_op jit(solution)/shard_map/dot_general | solution.py:164
  262.2 113.2 %all-to-all-done = bf16[16,32,4096]{2,1,0:T(8,128)(2,1)} async-done(((bf16[16,32,4096]{2,1,0:T(8,128)(2,1)}), bf16[16,32,4096]{2,1,0:T(8,128)(2,1)}, u32[]{:S(2)}, u32[]{:S(2)}) %all-to-all-start) | async-done | bytes 4194336 | tf_op jit(solution)/shard_map/all_to_all | solution.py:36
  375.3 8.2 %all-to-all-start.1 = ((bf16[16,32,4096]{2,1,0:T(8,128)(2,1)}), bf16[16,32,4096]{2,1,0:T(8,128)(2,1)}, u32[]{:S(2)}, u32[]{:S(2)}) async-start(bf16[16,32,4096]{2,1,0:T(8,128)(2,1)} %bitcast.153), calls=%async_computation.1 | async-start | bytes 8388608 | tf_op jit(solution)/shard_map/all_to_all | solution.py:36
  387.4 3.7 reshape.148
  393.6 62.8 %all-reduce.4 = (f32[3,3,256]{2,0,1:T(4,128)S(1)}, f32[128,16]{0,1:T(8,128)}) all-reduce(f32[3,3,256]{2,0,1:T(4,128)S(1)} %pad_maximum_fusion.4, f32[128,16]{0,1:T(8,128)S(1)} %bitcast.159), channel_id=1, replica_groups=mesh['dp'=2,'context'=8,'tensor'=16] {'dp','context'}, use_global_device_ids=true, to_apply=%region_9.10 | all-reduce | flops 4352 | bytes 34816 | tf_op jit(solution)/shard_map/psum | solution.py:149
  (139 shorter events, 79.4 us)
Async XLA Ops:
  7.2 99.0 %all-gather.4.cloned.1.call-start = ((), (), s32[]{:S(2)}) async-start(), calls=%async_computation.4 | async-start | bytes 4456448 | tf_op jit(solution)/shard_map/all_gather | solution.py:94
  11.1 139.5 %all-gather.6.cloned.1.call-start = ((), (), s32[]{:S(2)}) async-start(), calls=%async_computation.7 | async-start | bytes 4456448 | tf_op jit(solution)/shard_map/all_gather | solution.py:121
  11.9 6.8 %copy-start.21 = (f32[3,3,256]{2,1,0:T(4,128)S(1)}, f32[3,3,256]{2,1,0:T(4,128)}, u32[]{:S(2)}) copy-start(f32[3,3,256]{2,1,0:T(4,128)} %param.9) | copy-start | bytes 27652
  11.9 452.4 %reduce-scatter.5.cloned.1.call-start = ((), (), s32[]{:S(2)}) async-start(), calls=%async_computation.6 | async-start | bytes 2228224 | tf_op jit(solution)/shard_map/reduce_scatter | solution.py:158
  16.7 85.3 %collective-permute-start = (bf16[2048,3,256]{0,2,1:T(8,128)(2,1)}, bf16[2048,3,256]{0,2,1:T(8,128)(2,1)}, u32[]{:S(2)}, u32[]{:S(2)}) collective-permute-start(bf16[2048,3,256]{0,2,1:T(8,128)(2,1)} %copy.21), channel_id=1, source_target_pairs={{0,128},{128,0},{1,129},{129,1},{2,130},{130,2},{3,131},{131,3},{4... | collective-permute-start | bytes 9437192 | tf_op jit(solution)/shard_map/ppermute | solution.py:20
  17.5 108.7 %collective-permute-start.3 = (bf16[256,2048]{1,0:T(8,128)(2,1)}, bf16[256,2048]{1,0:T(8,128)(2,1)}, u32[]{:S(2)}, u32[]{:S(2)}) collective-permute-start(bf16[256,2048]{1,0:T(8,128)(2,1)} %param.8), channel_id=1, source_target_pairs={{0,128},{128,0},{1,129},{129,1},{2,130},{130,2},{3,131},{131,3},{4... | collective-permute-start | bytes 3145736 | tf_op jit(solution)/shard_map/ppermute | solution.py:20
  113.7 15.3 %copy-start.6 = (bf16[512,768]{1,0:T(8,128)(2,1)}, bf16[512,768]{1,0:T(8,128)(2,1)S(1)}, u32[]{:S(2)}) copy-start(bf16[512,768]{1,0:T(8,128)(2,1)S(1)} %convolution_convert_fusion.3) | copy-start | bytes 2359300
  113.9 15.1 %collective-permute-start.1 = (bf16[2,3,256]{0,2,1:T(8,128)(2,1)S(1)}, bf16[2,3,256]{0,2,1:T(8,128)(2,1)}, u32[]{:S(2)}, u32[]{:S(2)}) collective-permute-start(bf16[2,3,256]{0,2,1:T(8,128)(2,1)S(1)} %bitcast.156), channel_id=1, source_target_pairs={{0,16},{16,32},{32,48},{48,64},{64,80},{80,96},{96,112},{1,17},{17... | collective-permute-start | bytes 9224 | tf_op jit(solution)/shard_map/ppermute | solution.py:12
  134.2 22.4 %copy-start.19 = (f32[128,16]{0,1:T(8,128)S(1)}, f32[128,16]{0,1:T(8,128)}, u32[]{:S(2)}) copy-start(f32[128,16]{0,1:T(8,128)} %param.10) | copy-start | bytes 24580
  155.1 10.9 %copy-start.8 = (bf16[512,256]{0,1:T(8,128)(2,1)}, bf16[512,256]{0,1:T(8,128)(2,1)S(1)}, u32[]{:S(2)}) copy-start(bf16[512,256]{0,1:T(8,128)(2,1)S(1)} %get-tuple-element.17) | copy-start | bytes 786436
  155.1 13.7 %collective-permute-start.4 = (bf16[127,256]{0,1:T(8,128)(2,1)S(1)}, bf16[127,256]{0,1:T(8,128)(2,1)S(1)}, u32[]{:S(2)}, u32[]{:S(2)}) collective-permute-start(bf16[127,256]{0,1:T(8,128)(2,1)S(1)} %slice.125), channel_id=1, source_target_pairs={{16,0},{32,16},{48,32},{64,48},{80,64},{96,80},{112,96},{17,1},{33... | collective-permute-start | bytes 195080 | tf_op jit(solution)/shard_map/ppermute | solution.py:12
  181.0 16.6 %collective-permute-start.2 = (bf16[127,256]{0,1:T(8,128)(2,1)}, bf16[127,256]{0,1:T(8,128)(2,1)}, u32[]{:S(2)}, u32[]{:S(2)}) collective-permute-start(bf16[127,256]{0,1:T(8,128)(2,1)} %slice_bitcast_fusion.1), channel_id=1, source_target_pairs={{0,16},{16,32},{32,48},{48,64},{64,80},{80,96},{96,112},{1,17},{17... | collective-permute-start | bytes 195080 | tf_op jit(solution)/shard_map/ppermute | solution.py:12
  207.6 4.6 copy-start.11
  207.6 7.3 %copy-start.4 = (bf16[1,512,4096]{2,1,0:T(8,128)(2,1)S(1)}, bf16[1,512,4096]{2,1,0:T(8,128)(2,1)}, u32[]{:S(2)}) copy-start(bf16[1,512,4096]{2,1,0:T(8,128)(2,1)} %all-gather.6.cloned.1.call-done) | copy-start | bytes 12582916
  217.5 246.8 %reduce-scatter.3.cloned.1.call-start = ((), (), s32[]{:S(2)}) async-start(), calls=%async_computation.5 | async-start | bytes 6684672 | tf_op jit(solution)/shard_map/reduce_scatter | solution.py:155
  217.6 15.8 %copy-start.1 = (f32[512,1,256]{0,2,1:T(8,128)S(1)}, f32[512,1,256]{0,2,1:T(8,128)}, u32[]{:S(2)}) copy-start(f32[512,1,256]{0,2,1:T(8,128)} %get-tuple-element.24) | copy-start | bytes 1572868
  218.9 14.6 %copy-start = (f32[512,768]{0,1:T(8,128)S(1)}, f32[512,768]{0,1:T(8,128)}, u32[]{:S(2)}) copy-start(f32[512,768]{0,1:T(8,128)} %copy.23) | copy-start | bytes 4718596
  218.9 14.4 %collective-permute-start.5 = (f32[2,3,256]{0,2,1:T(8,128)S(1)}, f32[2,3,256]{0,2,1:T(8,128)S(1)}, u32[]{:S(2)}, u32[]{:S(2)}) collective-permute-start(f32[2,3,256]{0,2,1:T(8,128)S(1)} %slice.128), channel_id=1, source_target_pairs={{16,0},{32,16},{48,32},{64,48},{80,64},{96,80},{112,96},{17,1},{33... | collective-permute-start | bytes 18440 | tf_op jit(solution)/shard_map/ppermute | solution.py:12
  233.5 4.3 copy-start.25
  247.5 6.9 %copy-start.18 = (bf16[512,3,256]{0,2,1:T(8,128)(2,1)S(1)}, bf16[512,3,256]{0,2,1:T(8,128)(2,1)}, u32[]{:S(2)}) copy-start(bf16[512,3,256]{0,2,1:T(8,128)(2,1)} %copy-done.17) | copy-start | bytes 2359300
  247.5 127.9 %all-to-all-start = ((bf16[16,32,4096]{2,1,0:T(8,128)(2,1)}), bf16[16,32,4096]{2,1,0:T(8,128)(2,1)}, u32[]{:S(2)}, u32[]{:S(2)}) async-start(bf16[16,32,4096]{2,1,0:T(8,128)(2,1)} %bitcast.143), calls=%async_computation | async-start | bytes 8388608 | tf_op jit(solution)/shard_map/all_to_all | solution.py:36
  375.3 8.2 %copy-start.9 = (bf16[512,256]{0,1:T(8,128)(2,1)S(1)}, bf16[512,256]{0,1:T(8,128)(2,1)}, u32[]{:S(2)}) copy-start(bf16[512,256]{0,1:T(8,128)(2,1)} %copy-done.8) | copy-start | bytes 786436
  375.3 8.2 %copy-start.3 = (f32[4,256,16,16]{1,3,0,2:T(8,128)S(1)}, f32[4,256,16,16]{1,3,0,2:T(8,128)}, u32[]{:S(2)}) copy-start(f32[4,256,16,16]{1,3,0,2:T(8,128)} %copy_dynamic-update-slice_fusion) | copy-start | bytes 3145732
  375.3 84.7 %all-to-all-start.1 = ((bf16[16,32,4096]{2,1,0:T(8,128)(2,1)}), bf16[16,32,4096]{2,1,0:T(8,128)(2,1)}, u32[]{:S(2)}, u32[]{:S(2)}) async-start(bf16[16,32,4096]{2,1,0:T(8,128)(2,1)} %bitcast.153), calls=%async_computation.1 | async-start | bytes 8388608 | tf_op jit(solution)/shard_map/all_to_all | solution.py:36
  (16 other events, 31.1 us)
Sparse Core Ops, SparseCore 0:
  11.3 75.7 all-gather.3
  89.8 60.7 all-gather.5
  217.6 73.3 reduce-scatter.4
  294.0 83.9 reduce-scatter.2
where the time goes:
time: 472 us; the launch traced here: 471 us
  waiting for transfers between devices  225 us (48%)
  local copies, waits for them, and re-layouts  71.6 us (15%)
  blocking collectives  62.8 us (13%)
  matrix products  40.4 us (9%)
  starting transfers between devices  30.1 us (6%)
  other arithmetic  26.6 us (6%)
  between operations  14.2 us (3%)
    all_to_all x2, waiting for transfers between devices, scatter_sum(): pieces = lax.all_to_all(value.reshape(split), axis, dim, 0)  113 us
    ppermute x2, waiting for transfers between devices, pair_gather(): lax.ppermute(value, axis, [(i, (i + step) % count) for i in range(count)])  82.2 us
    psum x1, blocking collectives, per_device(): lax.psum((short_term, mixer_term), ('dp', 'context'))  62.8 us
    all_gather x1, waiting for transfers between devices, per_device(): cot_slab = lax.all_gather(cotangent[0], 'tensor', axis=0, tiled=True)  16.4 us
    unnamed x60, local copies, waits for them, and re-layouts  16.3 us
    all_to_all x2, starting transfers between devices, scatter_sum(): pieces = lax.all_to_all(value.reshape(split), axis, dim, 0)  15.1 us
    ppermute x4, starting transfers between devices, from_behind(): lax.ppermute(value, axis, [(source, source + steps) for source in range(i...  12.9 us
    ppermute x4, waiting for transfers between devices, from_behind(): lax.ppermute(value, axis, [(source, source + steps) for source in range(i...  12.7 us
  transfers between devices with their start and end apart: 12, of which 5 were waited for; matrix products, arithmetic and copies ran while one was open for 20% of the time, Pallas kernels for 0%

commit v1 on v0

--- a/solution.py
+++ b/solution.py
@@ -118,7 +118,9 @@
         0,
     )
     block_out = (own + branch).astype(jnp.bfloat16)[None]
-    cot_slab = lax.all_gather(cotangent[0], "tensor", axis=0, tiled=True)
+    cot_slab = jnp.concatenate(
+        lax.all_to_all(jnp.stack([cotangent[0]] * lax.axis_size("tensor")), "tensor", 0, 0), axis=0
+    )
     grad_rows = lax.dot_general(
         cot_slab, full_out, (((1,), (1,)), ((), ())), preferred_element_type=jnp.float32
     )

time: 472 us -> 496 us (1.051)
  waiting for transfers between devices: 225 us -> 238 us
  starting transfers between devices: 30.1 us -> 36.9 us
    ppermute x2, waiting for transfers between devices: 82.2 us -> 115 us  [pair_gather(): lax.ppermute(value, axis, [(i, (i + step) % count) for i in range(count)])]
    all_gather x1 -> x0, waiting for transfers between devices: 16.4 us -> none  [per_device(): cot_slab = lax.all_gather(cotangent[0], 'tensor', axis=0, tiled=True)]
    all_to_all x0 -> x1, starting transfers between devices: none -> 7.58 us  [per_device(): lax.all_to_all(jnp.stack([cotangent[0]] * lax.axis_size('tensor')), 'tens...]
    unnamed x60 -> x52, local copies, waits for them, and re-layouts: 16.3 us -> 13.9 us
  transfers between devices with their start and end apart: 12 -> 12, of which waited for: 5 -> 4; matrix products, arithmetic and copies ran while one was open for 20% -> 19% of each run, Pallas kernels for 0% -> 0%
where the time goes in v1:
time: 496 us; the launch traced here: 494 us
  waiting for transfers between devices  238 us (48%)
  local copies, waits for them, and re-layouts  69.1 us (14%)
  blocking collectives  66.6 us (13%)
  matrix products  43.9 us (9%)
  starting transfers between devices  36.9 us (7%)
  other arithmetic  25.6 us (5%)
  between operations  14.2 us (3%)
    ppermute x2, waiting for transfers between devices, pair_gather(): lax.ppermute(value, axis, [(i, (i + step) % count) for i in range(count)])  115 us
    all_to_all x2, waiting for transfers between devices, scatter_sum(): pieces = lax.all_to_all(value.reshape(split), axis, dim, 0)  113 us
    psum x1, blocking collectives, per_device(): lax.psum((short_term, mixer_term), ('dp', 'context'))  66.6 us
    all_to_all x2, starting transfers between devices, scatter_sum(): pieces = lax.all_to_all(value.reshape(split), axis, dim, 0)  14.8 us
    unnamed x52, local copies, waits for them, and re-layouts  13.9 us
    ppermute x4, starting transfers between devices, from_behind(): lax.ppermute(value, axis, [(source, source + steps) for source in range(i...  12.3 us
    another operation x4, local copies, waits for them, and re-layouts, skew_table(): jnp.tile(padded[:, None, :], (1, span, 1))  11.6 us
    dynamic_update_slice x4, local copies, waits for them, and re-layouts, pair_gather(): full = lax.dynamic_update_slice(full, part, start)  10.7 us
  transfers between devices with their start and end apart: 12, of which 4 were waited for; matrix products, arithmetic and copies ran while one was open for 19% of the time, Pallas kernels for 0%

profile of v1, /device:TPU:6, one launch (start us, length us, event | category | flops | bytes accessed | tf_op | source)
XLA Modules:
  0.0 493.9 jit_solution(9462856654877208316)
XLA Ops:
  11.2 4.7 copy.21
  19.3 7.6 %all-to-all-start.1 = ((bf16[16,32,4096]{2,1,0:T(8,128)(2,1)}), bf16[16,32,4096]{2,1,0:T(8,128)(2,1)}, u32[]{:S(2)}, u32[]{:S(2)}) async-start(bf16[16,32,4096]{2,1,0:T(8,128)(2,1)} %stack.25), calls=%async_computation.1 | async-start | bytes 8388608 | tf_op jit(solution)/shard_map/all_to_all | solution.py:122
  33.3 4.0 constant_dynamic-update-slice_fusion.3
  37.4 63.9 %collective-permute-done = bf16[2048,3,256]{0,2,1:T(8,128)(2,1)} collective-permute-done((bf16[2048,3,256]{0,2,1:T(8,128)(2,1)}, bf16[2048,3,256]{0,2,1:T(8,128)(2,1)}, u32[]{:S(2)}, u32[]{:S(2)}) %collective-permute-start) | collective-permute-done | bytes 3145760 | tf_op jit(solution)/shard_map/ppermute | solution.py:20
  101.3 4.1 constant_dynamic-update-slice_fusion.2
  105.4 7.5 %convolution_convert_fusion.3 = bf16[512,768]{1,0:T(8,128)(2,1)S(1)} fusion(bf16[512,4096]{1,0:T(8,128)(2,1)} %all-gather.2.cloned.1.call-done, bf16[4096,768]{0,1:T(8,128)(2,1)} %bitcast.1), kind=kOutput, calls=%fused_computation.26 | convolution fusion | flops 3221618688 | bytes 11272192 | tf_op jit(solution)/shard_map/dot_general | solution.py:99
  113.1 4.5 collective-permute-start.1
  117.6 50.9 %collective-permute-done.3 = bf16[256,2048]{1,0:T(8,128)(2,1)} collective-permute-done((bf16[256,2048]{1,0:T(8,128)(2,1)}, bf16[256,2048]{1,0:T(8,128)(2,1)}, u32[]{:S(2)}, u32[]{:S(2)}) %collective-permute-start.3) | collective-permute-done | bytes 1048608 | tf_op jit(solution)/shard_map/ppermute | solution.py:20
  172.2 4.2 multiply_add_fusion
  176.5 4.4 fusion.40
  184.4 3.9 tile.17
  198.7 3.9 fusion.12
  206.2 4.5 collective-permute-start.2
  212.8 3.9 tile.15
  228.1 4.2 fusion.9
  233.5 5.1 %convolution_convert_fusion.2 = bf16[256,4096]{1,0:T(8,128)(2,1)} fusion(bf16[512,4096]{1,0:T(8,128)(2,1)} %bitcast.13, f32[512,1,256]{0,2,1:T(8,128)} %reshape.155, f32[512,3,256]{0,2,1:T(8,128)} %multiply_add_fusion), kind=kOutput, calls=%fused_computation.5 | convolution fusion | flops 1075052544 | bytes 7340032 | tf_op jit(solution)/shard_map/dot_general | solution.py:127
  243.0 10.2 %collective-permute-done.5 = f32[2,3,256]{0,2,1:T(8,128)S(1)} collective-permute-done((f32[2,3,256]{0,2,1:T(8,128)S(1)}, f32[2,3,256]{0,2,1:T(8,128)S(1)}, u32[]{:S(2)}, u32[]{:S(2)}) %collective-permute-start.5) | collective-permute-done | bytes 6176 | tf_op jit(solution)/shard_map/ppermute | solution.py:12
  257.7 5.4 %convolution_convert_fusion = bf16[4096,3,256]{2,0,1:T(8,128)(2,1)} fusion(bf16[512,4096]{1,0:T(8,128)(2,1)S(1)} %copy-done.21, bf16[512,3,256]{0,2,1:T(8,128)(2,1)S(1)} %get-tuple-element.20), kind=kOutput, calls=%fused_computation.3 | convolution fusion | flops 3224371200 | bytes 11272192 | tf_op jit(solution)/shard_map/dot_general | solution.py:153
  263.1 4.4 convolution_convert_fusion.1
  267.5 7.3 %all-to-all-start = ((bf16[16,32,4096]{2,1,0:T(8,128)(2,1)}), bf16[16,32,4096]{2,1,0:T(8,128)(2,1)}, u32[]{:S(2)}, u32[]{:S(2)}) async-start(bf16[16,32,4096]{2,1,0:T(8,128)(2,1)} %bitcast.142), calls=%async_computation | async-start | bytes 8388608 | tf_op jit(solution)/shard_map/all_to_all | solution.py:36
  274.8 7.9 %bitcast_convert_fusion = bf16[512,4096]{1,0:T(8,128)(2,1)} fusion(bf16[512,3,256]{0,2,1:T(8,128)(2,1)S(1)} %copy-done.13, bf16[4096,3,256]{0,2,1:T(8,128)(2,1)} %constant_dynamic-update-slice_fusion.2), kind=kOutput, calls=%fused_computation | convolution fusion | flops 3223322624 | bytes 11272192 | tf_op jit(solution)/shard_map/dot_general | solution.py:166
  282.7 112.5 %all-to-all-done = bf16[16,32,4096]{2,1,0:T(8,128)(2,1)} async-done(((bf16[16,32,4096]{2,1,0:T(8,128)(2,1)}), bf16[16,32,4096]{2,1,0:T(8,128)(2,1)}, u32[]{:S(2)}, u32[]{:S(2)}) %all-to-all-start) | async-done | bytes 4194336 | tf_op jit(solution)/shard_map/all_to_all | solution.py:36
  395.2 7.5 %all-to-all-start.2 = ((bf16[16,32,4096]{2,1,0:T(8,128)(2,1)}), bf16[16,32,4096]{2,1,0:T(8,128)(2,1)}, u32[]{:S(2)}, u32[]{:S(2)}) async-start(bf16[16,32,4096]{2,1,0:T(8,128)(2,1)} %bitcast.154), calls=%async_computation.2 | async-start | bytes 8388608 | tf_op jit(solution)/shard_map/all_to_all | solution.py:36
  412.8 66.6 %all-reduce.4 = (f32[3,3,256]{2,0,1:T(4,128)S(1)}, f32[128,16]{0,1:T(8,128)}) all-reduce(f32[3,3,256]{2,0,1:T(4,128)S(1)} %pad_maximum_fusion.4, f32[128,16]{0,1:T(8,128)S(1)} %bitcast.160), channel_id=1, replica_groups=mesh['dp'=2,'context'=8,'tensor'=16] {'dp','context'}, use_global_device_ids=true, to_apply=%region_9.10 | all-reduce | flops 4352 | bytes 34816 | tf_op jit(solution)/shard_map/psum | solution.py:151
  (132 shorter events, 76.4 us)
Async XLA Ops:
  7.2 98.2 %all-gather.2.cloned.1.call-start = ((), (), s32[]{:S(2)}) async-start(), calls=%async_computation.5 | async-start | bytes 4456448 | tf_op jit(solution)/shard_map/all_gather | solution.py:94
  11.2 5.6 %copy-start.10 = (bf16[1,32,4096]{2,1,0:T(8,128)(2,1)S(1)}, bf16[1,32,4096]{2,1,0:T(8,128)(2,1)}, u32[]{:S(2)}) copy-start(bf16[1,32,4096]{2,1,0:T(8,128)(2,1)} %param.11) | copy-start | bytes 786436
  16.0 85.3 %collective-permute-start = (bf16[2048,3,256]{0,2,1:T(8,128)(2,1)}, bf16[2048,3,256]{0,2,1:T(8,128)(2,1)}, u32[]{:S(2)}, u32[]{:S(2)}) collective-permute-start(bf16[2048,3,256]{0,2,1:T(8,128)(2,1)} %copy.21), channel_id=1, source_target_pairs={{0,128},{128,0},{1,129},{129,1},{2,130},{130,2},{3,131},{131,3},{4... | collective-permute-start | bytes 9437192 | tf_op jit(solution)/shard_map/ppermute | solution.py:20
  19.3 8.9 %copy-start.17 = (f32[3,3,256]{2,1,0:T(4,128)S(1)}, f32[3,3,256]{2,1,0:T(4,128)}, u32[]{:S(2)}) copy-start(f32[3,3,256]{2,1,0:T(4,128)} %param.9) | copy-start | bytes 27652
  19.3 157.1 %all-to-all-start.1 = ((bf16[16,32,4096]{2,1,0:T(8,128)(2,1)}), bf16[16,32,4096]{2,1,0:T(8,128)(2,1)}, u32[]{:S(2)}, u32[]{:S(2)}) async-start(bf16[16,32,4096]{2,1,0:T(8,128)(2,1)} %stack.25), calls=%async_computation.1 | async-start | bytes 8388608 | tf_op jit(solution)/shard_map/all_to_all | solution.py:122
  26.9 460.4 %reduce-scatter.5.cloned.1.call-start = ((), (), s32[]{:S(2)}) async-start(), calls=%async_computation.7 | async-start | bytes 2228224 | tf_op jit(solution)/shard_map/reduce_scatter | solution.py:160
  27.0 141.5 %collective-permute-start.3 = (bf16[256,2048]{1,0:T(8,128)(2,1)}, bf16[256,2048]{1,0:T(8,128)(2,1)}, u32[]{:S(2)}, u32[]{:S(2)}) collective-permute-start(bf16[256,2048]{1,0:T(8,128)(2,1)} %param.8), channel_id=1, source_target_pairs={{0,128},{128,0},{1,129},{129,1},{2,130},{130,2},{3,131},{131,3},{4... | collective-permute-start | bytes 3145736 | tf_op jit(solution)/shard_map/ppermute | solution.py:20
  112.9 58.4 %copy-start.5 = (bf16[512,768]{1,0:T(8,128)(2,1)}, bf16[512,768]{1,0:T(8,128)(2,1)S(1)}, u32[]{:S(2)}) copy-start(bf16[512,768]{1,0:T(8,128)(2,1)S(1)} %convolution_convert_fusion.3) | copy-start | bytes 2359300
  113.1 58.2 %collective-permute-start.1 = (bf16[2,3,256]{0,2,1:T(8,128)(2,1)S(1)}, bf16[2,3,256]{0,2,1:T(8,128)(2,1)}, u32[]{:S(2)}, u32[]{:S(2)}) collective-permute-start(bf16[2,3,256]{0,2,1:T(8,128)(2,1)S(1)} %bitcast.157), channel_id=1, source_target_pairs={{0,16},{16,32},{32,48},{48,64},{64,80},{80,96},{96,112},{1,17},{17... | collective-permute-start | bytes 9224 | tf_op jit(solution)/shard_map/ppermute | solution.py:12
  176.5 6.0 %copy-start.14 = (f32[128,16]{0,1:T(8,128)S(1)}, f32[128,16]{0,1:T(8,128)}, u32[]{:S(2)}) copy-start(f32[128,16]{0,1:T(8,128)} %param.10) | copy-start | bytes 24580
  180.9 10.9 %copy-start.7 = (bf16[512,256]{0,1:T(8,128)(2,1)}, bf16[512,256]{0,1:T(8,128)(2,1)S(1)}, u32[]{:S(2)}) copy-start(bf16[512,256]{0,1:T(8,128)(2,1)S(1)} %get-tuple-element.17) | copy-start | bytes 786436
  180.9 13.8 %collective-permute-start.4 = (bf16[127,256]{0,1:T(8,128)(2,1)S(1)}, bf16[127,256]{0,1:T(8,128)(2,1)S(1)}, u32[]{:S(2)}, u32[]{:S(2)}) collective-permute-start(bf16[127,256]{0,1:T(8,128)(2,1)S(1)} %slice.125), channel_id=1, source_target_pairs={{16,0},{32,16},{48,32},{64,48},{80,64},{96,80},{112,96},{17,1},{33... | collective-permute-start | bytes 195080 | tf_op jit(solution)/shard_map/ppermute | solution.py:12
  203.8 7.0 %copy-start.15 = (f32[128,16]{0,1:T(8,128)S(1)}, f32[128,16]{0,1:T(8,128)}, u32[]{:S(2)}) copy-start(f32[128,16]{0,1:T(8,128)} %param.10) | copy-start | bytes 24580
  206.2 14.0 %collective-permute-start.2 = (bf16[127,256]{0,1:T(8,128)(2,1)S(1)}, bf16[127,256]{0,1:T(8,128)(2,1)S(1)}, u32[]{:S(2)}, u32[]{:S(2)}) collective-permute-start(bf16[127,256]{0,1:T(8,128)(2,1)S(1)} %slice_bitcast_fusion), channel_id=1, source_target_pairs={{0,16},{16,32},{32,48},{48,64},{64,80},{80,96},{96,112},{1,17},{17... | collective-permute-start | bytes 195080 | tf_op jit(solution)/shard_map/ppermute | solution.py:12
  238.7 248.7 %reduce-scatter.3.cloned.1.call-start = ((), (), s32[]{:S(2)}) async-start(), calls=%async_computation.6 | async-start | bytes 6684672 | tf_op jit(solution)/shard_map/reduce_scatter | solution.py:157
  239.8 13.3 %copy-start.1 = (f32[512,1,256]{0,2,1:T(8,128)S(1)}, f32[512,1,256]{0,2,1:T(8,128)}, u32[]{:S(2)}) copy-start(f32[512,1,256]{0,2,1:T(8,128)} %get-tuple-element.19) | copy-start | bytes 1572868
  241.2 12.1 %copy-start = (f32[512,768]{0,1:T(8,128)S(1)}, f32[512,768]{0,1:T(8,128)}, u32[]{:S(2)}) copy-start(f32[512,768]{0,1:T(8,128)} %copy.23) | copy-start | bytes 4718596
  241.2 12.0 %collective-permute-start.5 = (f32[2,3,256]{0,2,1:T(8,128)S(1)}, f32[2,3,256]{0,2,1:T(8,128)S(1)}, u32[]{:S(2)}, u32[]{:S(2)}) collective-permute-start(f32[2,3,256]{0,2,1:T(8,128)S(1)} %slice.128), channel_id=1, source_target_pairs={{16,0},{32,16},{48,32},{64,48},{80,64},{96,80},{112,96},{17,1},{33... | collective-permute-start | bytes 18440 | tf_op jit(solution)/shard_map/ppermute | solution.py:12
  253.3 4.3 copy-start.21
  267.5 7.3 %copy-start.13 = (bf16[512,3,256]{0,2,1:T(8,128)(2,1)S(1)}, bf16[512,3,256]{0,2,1:T(8,128)(2,1)}, u32[]{:S(2)}) copy-start(bf16[512,3,256]{0,2,1:T(8,128)(2,1)} %copy-done.12) | copy-start | bytes 2359300
  267.5 127.7 %all-to-all-start = ((bf16[16,32,4096]{2,1,0:T(8,128)(2,1)}), bf16[16,32,4096]{2,1,0:T(8,128)(2,1)}, u32[]{:S(2)}, u32[]{:S(2)}) async-start(bf16[16,32,4096]{2,1,0:T(8,128)(2,1)} %bitcast.142), calls=%async_computation | async-start | bytes 8388608 | tf_op jit(solution)/shard_map/all_to_all | solution.py:36
  395.2 7.5 %copy-start.8 = (bf16[512,256]{0,1:T(8,128)(2,1)S(1)}, bf16[512,256]{0,1:T(8,128)(2,1)}, u32[]{:S(2)}) copy-start(bf16[512,256]{0,1:T(8,128)(2,1)} %copy-done.7) | copy-start | bytes 786436
  395.2 7.6 %copy-start.3 = (f32[4,256,16,16]{1,3,0,2:T(8,128)S(1)}, f32[4,256,16,16]{1,3,0,2:T(8,128)}, u32[]{:S(2)}) copy-start(f32[4,256,16,16]{1,3,0,2:T(8,128)} %copy_dynamic-update-slice_fusion) | copy-start | bytes 3145732
  395.2 87.8 %all-to-all-start.2 = ((bf16[16,32,4096]{2,1,0:T(8,128)(2,1)}), bf16[16,32,4096]{2,1,0:T(8,128)(2,1)}, u32[]{:S(2)}, u32[]{:S(2)}) async-start(bf16[16,32,4096]{2,1,0:T(8,128)(2,1)} %bitcast.154), calls=%async_computation.2 | async-start | bytes 8388608 | tf_op jit(solution)/shard_map/all_to_all | solution.py:36
  (12 other events, 26.8 us)
Sparse Core Ops, SparseCore 0:
  11.3 82.6 all-gather.1
  238.8 77.2 reduce-scatter.4
  319.2 84.1 reduce-scatter.2
